TPU v7x, 256 devices: a whole 4x4x8 slice. The times are simulated.
256 devices in a mesh: rows: 64 (over y_lo, z, x), blk: 4 (over y_hi, core).
Axes of the slice: x: 4, y: 4 (y_hi: 2, y_lo: 2; y = y_hi * 2 + y_lo), z: 8, core: 2. Of those that a mesh axis runs over, the one named last changes fastest.
Arguments:
- block_weight: bfloat16 [64, 4, 4, 64, 128, 128], P('rows', 'blk'), may hold values from 0.049804688 to 50
- block_row: int32 [64, 4, 4, 64], P('rows', 'blk'), may hold values from 0 to 15, as said below
- block_col: int32 [64, 4, 4, 64], P('rows', 'blk'), may hold values from 0 to 7, as said below
- block_count: int32 [64, 4, 4], P('rows', 'blk'), may hold values from 1 to 64, as said below
- block_samples: int32 [64, 4, 4, 64], P('rows', 'blk'), may hold values from 1 to 8
- row_degree: float32 [64, 4, 2048], P('rows', 'blk'), may hold values from 0.125 to 8
- col_degree: float32 [4, 1024], P('blk', 'rows'), may hold values from 1 to 8
- test_matrix: bfloat16 [4, 1024, 128], P('blk', 'rows'), may hold values from -6 to 6
Outputs:
- basis: float32 [64, 4, 2048, 128], P('rows', 'blk')
- triangle: float32 [128, 128], replicated
Inputs may be any that keep to these rules, and one draw needn't show every extreme that they name: Within one band and slab, the slots k < 64 hold distinct (block_row, block_col) pairs. `block_col`: see block_row: pairs are distinct within one band and slab. `block_count`: some band and slab has all 64 slots live in every draw.
All inputs are finite; a program needn't handle non-finite values.
Results may differ from a plain program's by a relative error of at most 0.0065.
Values may be sent and summed in bfloat16 or wider, within the bound.
A program may use at most 64 MiB of HBM per device.

v0:
```python
import jax
import jax.numpy as jnp
from jax import lax
from jax.sharding import PartitionSpec as P

scale_factor = 16.0


def passed_along(block, axis, distance):
    devices = range(lax.axis_size(axis))
    route = [((i - distance) % len(devices), i) for i in devices]
    return lax.ppermute(block, axis, route)


def tile_update(
    running, weights, rows_idx, cols_idx, live_count, samples, row_deg, slab_rows, slab_deg
):
    block_edge = weights.shape[-1]
    capacity = weights.shape[0]
    band_blocks = running.shape[0]
    slab_blocks = slab_rows.shape[0] // block_edge
    slab_tiles = slab_rows.reshape(slab_blocks, block_edge, slab_rows.shape[1])
    picked = slab_tiles[cols_idx]
    col_d = slab_deg.reshape(slab_blocks, block_edge)[cols_idx]
    row_d = row_deg.reshape(band_blocks, block_edge)[rows_idx]
    scaled_ratio = (
        scale_factor
        * weights.astype(jnp.float32)
        / (samples.astype(jnp.float32)[:, None, None] * row_d[:, :, None] * col_d[:, None, :])
    )
    entries = jnp.log(jnp.maximum(scaled_ratio, 1.0)).astype(jnp.bfloat16)
    products = jnp.einsum("kij,kjc->kic", entries, picked, preferred_element_type=jnp.float32)
    alive_mask = (jnp.arange(capacity, dtype=jnp.int32) < live_count).astype(jnp.float32)
    chooser = (rows_idx[None, :] == jnp.arange(band_blocks, dtype=jnp.int32)[:, None]).astype(
        jnp.float32
    ) * alive_mask[None, :]
    return running + jnp.einsum("rk,kic->ric", chooser, products, precision=lax.Precision.HIGHEST)


def body(
    block_weight,
    block_row,
    block_col,
    block_count,
    block_samples,
    row_degree,
    col_degree,
    test_matrix,
):
    loop_size = lax.axis_size("blk")
    position = lax.axis_index("blk")
    weights_all = block_weight[0, 0]
    rows_all = block_row[0, 0]
    cols_all = block_col[0, 0]
    counts_all = block_count[0, 0]
    samples_all = block_samples[0, 0]
    row_deg = row_degree[0, 0]
    block_edge = weights_all.shape[-1]
    band_blocks = row_deg.shape[0] // block_edge
    running = jnp.zeros((band_blocks, block_edge, test_matrix.shape[2]), jnp.float32)
    piece_pair = (test_matrix, col_degree)
    for t in range(loop_size):
        if t > 0:
            piece_pair = (
                passed_along(piece_pair[0], "blk", 1),
                passed_along(piece_pair[1].astype(jnp.bfloat16), "blk", 1).astype(jnp.float32),
            )
        slab_rows, slab_deg = (
            lax.all_gather(piece_pair[0], "rows", axis=1, tiled=True),
            lax.all_gather(piece_pair[1].astype(jnp.bfloat16), "rows", axis=1, tiled=True).astype(
                jnp.float32
            ),
        )
        slab_index = (position - t) % loop_size
        apply_slab_rows = slab_rows[0]
        apply_slab_deg = slab_deg[0]
        slab_index = jnp.asarray(slab_index)
        running = tile_update(
            running,
            lax.dynamic_index_in_dim(weights_all, slab_index, 0, keepdims=False),
            lax.dynamic_index_in_dim(rows_all, slab_index, 0, keepdims=False),
            lax.dynamic_index_in_dim(cols_all, slab_index, 0, keepdims=False),
            lax.dynamic_index_in_dim(counts_all, slab_index, 0, keepdims=False),
            lax.dynamic_index_in_dim(samples_all, slab_index, 0, keepdims=False),
            row_deg,
            apply_slab_rows,
            apply_slab_deg,
        )
    flat_rows = running.reshape(band_blocks * block_edge, running.shape[2])
    gram_local = jnp.dot(
        flat_rows.T, flat_rows, precision=lax.Precision.HIGHEST, preferred_element_type=jnp.float32
    )
    gram_total = lax.psum(gram_local, ("rows", "blk"))
    lower_factor = jnp.linalg.cholesky(gram_total)
    total_rows = flat_rows.shape[0] * lax.axis_size("rows") * loop_size
    root = jnp.sqrt(jnp.float32(total_rows))
    basis_rows = (
        lax.linalg.triangular_solve(
            lower_factor, flat_rows, left_side=False, lower=True, transpose_a=True
        )
        * root
    )
    return (basis_rows.reshape(1, 1, flat_rows.shape[0], flat_rows.shape[1]), lower_factor.T / root)


def solution(mesh):
    placed = (
        P("rows", "blk", None, None, None, None),
        P("rows", "blk", None, None),
        P("rows", "blk", None, None),
        P("rows", "blk", None),
        P("rows", "blk", None, None),
        P("rows", "blk", None),
        P("blk", "rows"),
        P("blk", "rows", None),
    )
    return jax.shard_map(
        body,
        mesh=mesh,
        in_specs=placed,
        out_specs=(P("rows", "blk", None, None), P()),
        check_vma=False,
    )
```

profile of v0, /device:TPU:1, one launch (start us, length us, event | category | flops | bytes accessed | tf_op | source)
XLA Modules:
  0.0 1118.6 jit_solution(2050559915229179514)
XLA Ops:
  7.2 0.0 all-reduce.7.cloned.1.call-start
  7.2 4.4 collective-permute-start.1
  11.6 0.7 convert_bitcast_fusion
  12.3 0.0 collective-permute-start
  12.3 132.2 %all_gather.25 = bf16[1,1024,128]{2,1,0:T(8,128)(2,1)S(1)} all-gather(bf16[1,16,128]{2,1,0:T(8,128)(2,1)} %param.15), channel_id=1, replica_groups=mesh['rows'=64,'blk'=4] {'rows'}, dimensions={1}, use_global_device_ids=true | all-gather | bytes 266240 | tf_op jit(solution)/shard_map/all_gather | solution.py:69
  144.4 1.4 fusion.107
  145.9 0.8 fusion.90
  146.7 0.8 fusion.102
  147.6 1.4 constant_dynamic-slice_fusion.2
  149.0 0.6 compare_convert_fusion.2
  149.7 0.6 gather_fusion.3
  150.3 0.6 gather_fusion
  150.9 0.6 compare_convert_fusion.3
  151.6 0.6 gather_fusion.6
  152.2 1.1 compare_convert_fusion.1
  153.2 0.6 gather_fusion.9
  153.8 1.1 compare_convert_fusion
  155.0 1.3 dynamic-slice.20
  156.9 0.1 broadcast_multiply_fusion.2
  157.0 1.0 gather_fusion.2
  157.9 0.1 broadcast_multiply_fusion.3
  158.0 0.1 broadcast_multiply_fusion.1
  158.1 0.1 broadcast_multiply_fusion
  158.2 0.2 dynamic-update-slice.3
  158.4 0.2 dynamic-update-slice.4
  158.6 29.4 %collective-permute-start.2 = (bf16[1,16]{1,0:T(2,128)(2,1)S(1)}, bf16[1,16]{1,0:T(2,128)(2,1)S(1)}, u32[]{:S(2)}, u32[]{:S(2)}) collective-permute-start(bf16[1,16]{1,0:T(2,128)(2,1)S(1)} %collective-permute-done), channel_id=1, source_target_pairs={{3,0},{0,1},{1,2},{2,3},{7,4},{4,5},{5,6},{6,7},{11,8},{8,9},{9,10... | collective-permute-start | bytes 104 | tf_op jit(solution)/shard_map/ppermute | solution.py:12
  188.0 0.7 collective-permute-done.2
  188.7 0.2 dynamic-update-slice.5
  188.9 3.8 collective-permute-start.4
  192.7 0.7 collective-permute-done.4
  193.5 0.2 dynamic-update-slice.6
  193.6 127.1 %all-reduce.4 = (bf16[1024]{0:T(1024)(128)(2,1)S(1)}, bf16[1024]{0:T(1024)(128)(2,1)S(1)}, bf16[1024]{0:T(1024)(128)(2,1)S(1)}, bf16[1024]{0:T(1024)(128)(2,1)S(1)}) all-reduce(bf16[1024]{0:T(1024)(128)(2,1)S(1)} %dynamic-update-slice.4, bf16[1024]{0:T(1024)(128)(2,1)S(1)} %dynamic-update-slice.3, ...), channel_id=1, replica_groups=mesh['rows'=64,'blk'=4] {'rows'}, use_global_device_ids=true, to_apply=%add.1 | all-reduce | flops 4096 | bytes 16384
  320.8 0.6 gather_fusion.1
  321.4 4.1 fusion.21
  325.5 0.6 gather_fusion.4
  326.1 0.6 gather_fusion.7
  326.7 0.6 gather_fusion.10
  327.3 124.8 %all_gather.27 = bf16[1,1024,128]{2,1,0:T(8,128)(2,1)S(1)} all-gather(bf16[1,16,128]{2,1,0:T(8,128)(2,1)S(1)} %collective-permute-done.1), channel_id=1, replica_groups=mesh['rows'=64,'blk'=4] {'rows'}, dimensions={1}, use_global_device_ids=true | all-gather | bytes 266240 | tf_op jit(solution)/shard_map/all_gather | solution.py:69
  452.1 0.9 gather_fusion.5
  453.1 3.6 fusion.23
  456.7 4.4 fusion.16
  461.0 60.1 %collective-permute-start.3 = (bf16[1,16,128]{2,1,0:T(8,128)(2,1)S(1)}, bf16[1,16,128]{2,1,0:T(8,128)(2,1)S(1)}, u32[]{:S(2)}, u32[]{:S(2)}) collective-permute-start(bf16[1,16,128]{2,1,0:T(8,128)(2,1)S(1)} %collective-permute-done.1), channel_id=1, source_target_pairs={{3,0},{0,1},{1,2},{2,3},{7,4},{4,5},{5,6},{6,7},{11,8},{8,9},{9,10... | collective-permute-start | bytes 12296 | tf_op jit(solution)/shard_map/ppermute | solution.py:12
  521.1 4.4 fusion.49
  525.5 124.0 %all_gather.29 = bf16[1,1024,128]{2,1,0:T(8,128)(2,1)S(1)} all-gather(bf16[1,16,128]{2,1,0:T(8,128)(2,1)S(1)} %collective-permute-done.3), channel_id=1, replica_groups=mesh['rows'=64,'blk'=4] {'rows'}, dimensions={1}, use_global_device_ids=true | all-gather | bytes 266240 | tf_op jit(solution)/shard_map/all_gather | solution.py:69
  649.6 1.0 gather_fusion.8
  650.6 3.6 fusion.25
  654.2 27.5 %collective-permute-start.5 = (bf16[1,16,128]{2,1,0:T(8,128)(2,1)S(1)}, bf16[1,16,128]{2,1,0:T(8,128)(2,1)S(1)}, u32[]{:S(2)}, u32[]{:S(2)}) collective-permute-start(bf16[1,16,128]{2,1,0:T(8,128)(2,1)S(1)} %copy-done.3), channel_id=1, source_target_pairs={{3,0},{0,1},{1,2},{2,3},{7,4},{4,5},{5,6},{6,7},{11,8},{8,9},{9,10... | collective-permute-start | bytes 12296 | tf_op jit(solution)/shard_map/ppermute | solution.py:12
  681.8 4.4 fusion.52
  686.2 125.7 %all_gather.31 = bf16[1,1024,128]{2,1,0:T(8,128)(2,1)S(1)} all-gather(bf16[1,16,128]{2,1,0:T(8,128)(2,1)S(1)} %collective-permute-done.5), channel_id=1, replica_groups=mesh['rows'=64,'blk'=4] {'rows'}, dimensions={1}, use_global_device_ids=true | all-gather | bytes 266240 | tf_op jit(solution)/shard_map/all_gather | solution.py:69
  811.9 2.1 gather_fusion.11
  814.0 3.3 fusion.27
  817.4 4.4 fusion.55
  821.8 2.5 convolution_bitcast_fusion
  824.3 0.0 all-reduce.7.cloned.1.call-update
  824.4 0.3 copy.15
  824.7 259.5 %all-reduce.7.cloned.1.call-done = f32[128,128]{0,1:T(8,128)} async-done(((f32[128,128]{0,1:T(8,128)}), f32[128,128]{0,1:T(8,128)}) %all-reduce.7.cloned.1.call-update) | async-done | bytes 65552 | tf_op jit(solution)/shard_map/psum | solution.py:93
  1084.2 0.9 copy.19
  1085.1 0.9 fusion.59
  1086.0 11.7 %cholesky.16 = f32[128,128]{1,0:T(8,128)S(1)} custom-call(f32[128,128]{1,0:T(8,128)S(1)} %fusion.59), custom_call_target="Cholesky" | custom-call | tf_op jit(solution)/shard_map/jit(cholesky)/cholesky | solution.py:94
  1097.7 0.6 compare_reduce_fusion
  1098.4 0.7 multiply_bitcast_fusion
  1099.1 9.8 custom-call.6
  1108.9 0.7 copy.20
  1109.6 1.9 fusion.20
  (37 shorter events, 0.2 us)
Async XLA Ops:
  7.2 142.5 %copy-start = (f32[1,1,2048]{2,1,0:T(1,128)S(1)}, f32[1,1,2048]{2,1,0:T(1,128)}, u32[]{:S(2)}) copy-start(f32[1,1,2048]{2,1,0:T(1,128)} %param.13) | copy-start | bytes 24580
  7.2 1077.0 %all-reduce.7.cloned.1.call-start = ((), (), s32[]{:S(2)}) async-start(), calls=%async_computation | async-start | bytes 131072 | tf_op jit(solution)/shard_map/psum | solution.py:93
  7.2 320.1 %collective-permute-start.1 = (bf16[1,16,128]{2,1,0:T(8,128)(2,1)}, bf16[1,16,128]{2,1,0:T(8,128)(2,1)S(1)}, u32[]{:S(2)}, u32[]{:S(2)}) collective-permute-start(bf16[1,16,128]{2,1,0:T(8,128)(2,1)} %param.15), channel_id=1, source_target_pairs={{3,0},{0,1},{1,2},{2,3},{7,4},{4,5},{5,6},{6,7},{11,8},{8,9},{9,10... | collective-permute-start | bytes 12296 | tf_op jit(solution)/shard_map/ppermute | solution.py:12
  12.3 146.1 %collective-permute-start = (bf16[1,16]{1,0:T(2,128)(2,1)S(1)}, bf16[1,16]{1,0:T(2,128)(2,1)S(1)}, u32[]{:S(2)}, u32[]{:S(2)}) collective-permute-start(bf16[1,16]{1,0:T(2,128)(2,1)S(1)} %get-tuple-element.33), channel_id=1, source_target_pairs={{3,0},{0,1},{1,2},{2,3},{7,4},{4,5},{5,6},{6,7},{11,8},{8,9},{9,10... | collective-permute-start | bytes 104 | tf_op jit(solution)/shard_map/ppermute | solution.py:12
  158.6 30.1 %collective-permute-start.2 = (bf16[1,16]{1,0:T(2,128)(2,1)S(1)}, bf16[1,16]{1,0:T(2,128)(2,1)S(1)}, u32[]{:S(2)}, u32[]{:S(2)}) collective-permute-start(bf16[1,16]{1,0:T(2,128)(2,1)S(1)} %collective-permute-done), channel_id=1, source_target_pairs={{3,0},{0,1},{1,2},{2,3},{7,4},{4,5},{5,6},{6,7},{11,8},{8,9},{9,10... | collective-permute-start | bytes 104 | tf_op jit(solution)/shard_map/ppermute | solution.py:12
  188.9 4.5 collective-permute-start.4
  456.7 64.4 %copy-start.1 = (f32[64,128,128]{2,1,0:T(8,128)S(1)}, f32[64,128,128]{2,1,0:T(8,128)}, u32[]{:S(2)}) copy-start(f32[64,128,128]{2,1,0:T(8,128)} %fusion.21) | copy-start | bytes 12582916
  461.0 64.5 %collective-permute-start.3 = (bf16[1,16,128]{2,1,0:T(8,128)(2,1)S(1)}, bf16[1,16,128]{2,1,0:T(8,128)(2,1)S(1)}, u32[]{:S(2)}, u32[]{:S(2)}) collective-permute-start(bf16[1,16,128]{2,1,0:T(8,128)(2,1)S(1)} %collective-permute-done.1), channel_id=1, source_target_pairs={{3,0},{0,1},{1,2},{2,3},{7,4},{4,5},{5,6},{6,7},{11,8},{8,9},{9,10... | collective-permute-start | bytes 12296 | tf_op jit(solution)/shard_map/ppermute | solution.py:12
  525.5 124.0 %copy-start.2 = (bf16[1,16,128]{2,1,0:T(8,128)(2,1)}, bf16[1,16,128]{2,1,0:T(8,128)(2,1)S(1)}, u32[]{:S(2)}) copy-start(bf16[1,16,128]{2,1,0:T(8,128)(2,1)S(1)} %collective-permute-done.3) | copy-start | bytes 12292
  650.5 3.7 copy-start.3
  650.5 31.2 %copy-start.5 = (s32[64]{0:T(128)S(1)}, s32[64]{0:T(128)}, u32[]{:S(2)}) copy-start(s32[64]{0:T(128)} %get-tuple-element.15) | copy-start | bytes 772
  650.5 31.2 %copy-start.7 = (f32[64]{0:T(128)S(1)}, f32[64]{0:T(128)}, u32[]{:S(2)}) copy-start(f32[64]{0:T(128)} %compare_convert_fusion.1) | copy-start | bytes 772
  654.2 32.0 %collective-permute-start.5 = (bf16[1,16,128]{2,1,0:T(8,128)(2,1)S(1)}, bf16[1,16,128]{2,1,0:T(8,128)(2,1)S(1)}, u32[]{:S(2)}, u32[]{:S(2)}) collective-permute-start(bf16[1,16,128]{2,1,0:T(8,128)(2,1)S(1)} %copy-done.3), channel_id=1, source_target_pairs={{3,0},{0,1},{1,2},{2,3},{7,4},{4,5},{5,6},{6,7},{11,8},{8,9},{9,10... | collective-permute-start | bytes 12296 | tf_op jit(solution)/shard_map/ppermute | solution.py:12
  814.0 3.4 copy-start.4
  814.0 3.4 copy-start.6
Sparse Core Ops, SparseCore 0:
  824.5 259.6 all-reduce.6
where the time goes:
time: 1120 us
  blocking collectives  634 us (57%)
  waiting for transfers between devices  261 us (23%)
  starting transfers between devices  125 us (11%)
  matrix products  36.7 us (3%)
  other arithmetic  29.9 us (3%)
  local copies, waits for them, and re-layouts  16.8 us (2%)
  between operations  15.2 us (1%)
    all_gather x4, blocking collectives, body(): lax.all_gather(piece_pair[0], 'rows', axis=1, tiled=True)  507 us
    psum x1, waiting for transfers between devices, body(): gram_total = lax.psum(gram_local, ('rows', 'blk'))  260 us
    unnamed x1, blocking collectives  127 us
    ppermute x6, starting transfers between devices, passed_along(): return lax.ppermute(block, axis, route)  125 us
  transfers between devices with their start and end apart: 7, of which 3 were waited for; matrix products, arithmetic and copies ran while one was open for 3% of the time, Pallas kernels for 0%

commit v1 on v0

--- a/solution.py
+++ b/solution.py
@@ -2,6 +2,7 @@
 import jax.numpy as jnp
 from jax import lax
 from jax.sharding import PartitionSpec as P
+from jax.lax import all_to_all, axis_size
 
 scale_factor = 16.0
 
@@ -65,8 +66,20 @@
                 passed_along(piece_pair[0], "blk", 1),
                 passed_along(piece_pair[1].astype(jnp.bfloat16), "blk", 1).astype(jnp.float32),
             )
+
+        def shape_point_by_axis(axis_k, frame_in):
+            return jnp.concatenate(
+                all_to_all(
+                    jnp.stack([frame_in] * axis_size("rows")),
+                    axis_name="rows",
+                    split_axis=0,
+                    concat_axis=0,
+                ),
+                axis=axis_k,
+            )
+
         slab_rows, slab_deg = (
-            lax.all_gather(piece_pair[0], "rows", axis=1, tiled=True),
+            shape_point_by_axis(1, frame_in=piece_pair[0]),
             lax.all_gather(piece_pair[1].astype(jnp.bfloat16), "rows", axis=1, tiled=True).astype(
                 jnp.float32
             ),

time: 1120 us -> 582 us (0.52)
  blocking collectives: 634 us -> 132 us
  starting transfers between devices: 125 us -> 88.7 us
    all_gather x4 -> x0, blocking collectives: 507 us -> none  [body(): lax.all_gather(piece_pair[0], 'rows', axis=1, tiled=True)]
    ppermute x6, starting transfers between devices: 125 us -> 44.7 us  [passed_along(): return lax.ppermute(block, axis, route)]
    all_to_all x0 -> x4, starting transfers between devices: none -> 43.9 us  [shape_point_by_axis(): all_to_all(jnp.stack([frame_in] * axis_size('rows')), axis_name='rows', s...]
    psum x1, waiting for transfers between devices: 260 us -> 241 us  [body(): gram_total = lax.psum(gram_local, ('rows', 'blk'))]
  transfers between devices with their start and end apart: 7 -> 11, of which waited for: 3 -> 5; matrix products, arithmetic and copies ran while one was open for 3% -> 8% of each run, Pallas kernels for 0% -> 0%
where the time goes in v1:
time: 582 us; the launch traced here: 573 us
  waiting for transfers between devices  251 us (43%)
  blocking collectives  132 us (23%)
  starting transfers between devices  88.7 us (15%)
  matrix products  36.2 us (6%)
  other arithmetic  29 us (5%)
  local copies, waits for them, and re-layouts  21 us (4%)
  between operations  15.5 us (3%)
    psum x1, waiting for transfers between devices, body(): gram_total = lax.psum(gram_local, ('rows', 'blk'))  241 us
    unnamed x1, blocking collectives  132 us
    ppermute x6, starting transfers between devices, passed_along(): return lax.ppermute(block, axis, route)  44.7 us
    all_to_all x4, starting transfers between devices, shape_point_by_axis(): all_to_all(jnp.stack([frame_in] * axis_size('rows')), axis_name='rows', s...  43.9 us
    dot_general x4, matrix products, tile_update(): jnp.einsum('rk,kic->ric', chooser, products, precision=lax.Precision.HIGH...  17.6 us
    dot_general x4, matrix products, tile_update(): jnp.einsum('kij,kjc->kic', entries, picked, preferred_element_type=jnp.fl...  14.2 us
    another operation x3, other arithmetic, body(): lower_factor = jnp.linalg.cholesky(gram_total)  12.4 us
  transfers between devices with their start and end apart: 11, of which 5 were waited for; matrix products, arithmetic and copies ran while one was open for 8% of the time, Pallas kernels for 0%

profile of v1, /device:TPU:1, one launch (start us, length us, event | category | flops | bytes accessed | tf_op | source)
XLA Modules:
  0.0 573.5 jit_solution(11685440756327927550)
XLA Ops:
  7.2 4.4 collective-permute-start.1
  11.5 0.7 convert_bitcast_fusion
  12.2 1.4 stack.8
  13.6 11.8 %all-to-all-start = ((bf16[64,1,16,128]{3,2,1,0:T(8,128)(2,1)}), bf16[64,1,16,128]{3,2,1,0:T(8,128)(2,1)S(1)}, u32[]{:S(2)}, u32[]{:S(2)}) async-start(bf16[64,1,16,128]{3,2,1,0:T(8,128)(2,1)} %stack.8), calls=%async_computation | async-start | bytes 524288 | tf_op jit(solution)/shard_map/all_to_all | solution.py:72
  25.5 0.8 fusion.107
  26.4 0.8 fusion.90
  27.2 0.8 fusion.102
  28.1 1.5 constant_dynamic-slice_fusion.2
  29.5 0.6 compare_convert_fusion.2
  30.2 0.6 gather_fusion.3
  30.8 0.6 gather_fusion
  31.4 0.6 compare_convert_fusion.3
  32.1 0.6 gather_fusion.6
  32.7 0.6 compare_convert_fusion.1
  33.3 0.6 gather_fusion.9
  33.9 0.6 compare_convert_fusion
  34.6 1.3 dynamic-slice.20
  36.7 0.1 broadcast_multiply_fusion
  36.8 0.2 dynamic-update-slice.3
  37.1 0.2 dynamic-update-slice.4
  37.3 2.3 collective-permute-start.2
  39.5 0.7 collective-permute-done.2
  40.3 0.2 dynamic-update-slice.5
  40.4 3.8 collective-permute-start.4
  44.3 0.7 collective-permute-done.4
  45.0 0.2 dynamic-update-slice.6
  45.2 132.3 %all-reduce.4 = (bf16[1024]{0:T(1024)(128)(2,1)S(1)}, bf16[1024]{0:T(1024)(128)(2,1)S(1)}, bf16[1024]{0:T(1024)(128)(2,1)S(1)}, bf16[1024]{0:T(1024)(128)(2,1)S(1)}) all-reduce(bf16[1024]{0:T(1024)(128)(2,1)S(1)} %dynamic-update-slice.4, bf16[1024]{0:T(1024)(128)(2,1)S(1)} %dynamic-update-slice.3, ...), channel_id=1, replica_groups=mesh['rows'=64,'blk'=4] {'rows'}, use_global_device_ids=true, to_apply=%add.1 | all-reduce | flops 4096 | bytes 16384
  177.5 32.1 %collective-permute-start.3 = (bf16[1,16,128]{2,1,0:T(8,128)(2,1)S(1)}, bf16[1,16,128]{2,1,0:T(8,128)(2,1)S(1)}, u32[]{:S(2)}, u32[]{:S(2)}) collective-permute-start(bf16[1,16,128]{2,1,0:T(8,128)(2,1)S(1)} %collective-permute-done.1), channel_id=1, source_target_pairs={{3,0},{0,1},{1,2},{2,3},{7,4},{4,5},{5,6},{6,7},{11,8},{8,9},{9,10... | collective-permute-start | bytes 12296 | tf_op jit(solution)/shard_map/ppermute | solution.py:13
  209.6 0.6 gather_fusion.4
  210.2 0.6 gather_fusion.1
  210.8 0.6 gather_fusion.7
  211.4 0.6 gather_fusion.10
  212.0 2.1 collective-permute-start.5
  214.2 0.7 stack.9
  214.9 4.6 all-to-all-start.1
  219.5 1.0 gather_fusion.2
  220.5 4.1 fusion.21
  224.6 7.4 %all-to-all-done.1 = bf16[64,1,16,128]{3,2,1,0:T(8,128)(2,1)S(1)} async-done(((bf16[64,1,16,128]{3,2,1,0:T(8,128)(2,1)}), bf16[64,1,16,128]{3,2,1,0:T(8,128)(2,1)S(1)}, u32[]{:S(2)}, u32[]{:S(2)}) %all-to-all-start.1) | async-done | bytes 262176 | tf_op jit(solution)/shard_map/all_to_all | solution.py:72
  232.0 0.7 stack.10
  232.8 16.9 %all-to-all-start.2 = ((bf16[64,1,16,128]{3,2,1,0:T(8,128)(2,1)}), bf16[64,1,16,128]{3,2,1,0:T(8,128)(2,1)S(1)}, u32[]{:S(2)}, u32[]{:S(2)}) async-start(bf16[64,1,16,128]{3,2,1,0:T(8,128)(2,1)} %stack.10), calls=%async_computation.2 | async-start | bytes 524288 | tf_op jit(solution)/shard_map/all_to_all | solution.py:72
  249.7 1.0 gather_fusion.5
  250.6 3.6 fusion.23
  254.2 4.4 fusion.16
  258.6 4.4 fusion.49
  263.0 0.7 stack.11
  263.8 10.6 %all-to-all-start.3 = ((bf16[64,1,16,128]{3,2,1,0:T(8,128)(2,1)}), bf16[64,1,16,128]{3,2,1,0:T(8,128)(2,1)S(1)}, u32[]{:S(2)}, u32[]{:S(2)}) async-start(bf16[64,1,16,128]{3,2,1,0:T(8,128)(2,1)} %stack.11), calls=%async_computation.3 | async-start | bytes 524288 | tf_op jit(solution)/shard_map/all_to_all | solution.py:72
  274.5 2.2 gather_fusion.8
  276.6 3.1 fusion.25
  279.8 4.4 fusion.52
  284.2 1.1 all-to-all-done.3
  285.3 2.2 gather_fusion.11
  287.5 3.3 fusion.27
  290.8 4.4 fusion.55
  295.2 2.5 convolution_bitcast_fusion
  297.7 0.3 copy.15
  298.1 240.8 %all-reduce.7.cloned.1.call-done = f32[128,128]{0,1:T(8,128)} async-done(((f32[128,128]{0,1:T(8,128)}), f32[128,128]{0,1:T(8,128)}) %all-reduce.7.cloned.1.call-update) | async-done | bytes 65552 | tf_op jit(solution)/shard_map/psum | solution.py:106
  538.9 0.9 copy.19
  539.8 0.9 fusion.59
  540.7 11.7 %cholesky.16 = f32[128,128]{1,0:T(8,128)S(1)} custom-call(f32[128,128]{1,0:T(8,128)S(1)} %fusion.59), custom_call_target="Cholesky" | custom-call | tf_op jit(solution)/shard_map/jit(cholesky)/cholesky | solution.py:107
  552.4 0.6 compare_reduce_fusion
  553.1 0.7 multiply_bitcast_fusion
  553.7 9.8 %custom-call.6 = f32[1,128,128]{1,2,0:T(8,128)S(1)} custom-call(f32[1,128,128]{2,1,0:T(8,128)S(1)} %get-tuple-element.11), custom_call_target="InvertDiagBlocksLowerTriangular" | custom-call | tf_op jit(solution)/shard_map/triangular_solve | solution.py:111
  563.6 0.7 copy.20
  564.3 1.9 fusion.20
  (33 shorter events, 0.4 us)
Async XLA Ops:
  7.2 23.0 %copy-start = (f32[1,1,2048]{2,1,0:T(1,128)S(1)}, f32[1,1,2048]{2,1,0:T(1,128)}, u32[]{:S(2)}) copy-start(f32[1,1,2048]{2,1,0:T(1,128)} %param.13) | copy-start | bytes 24580
  7.2 170.3 %collective-permute-start.1 = (bf16[1,16,128]{2,1,0:T(8,128)(2,1)}, bf16[1,16,128]{2,1,0:T(8,128)(2,1)S(1)}, u32[]{:S(2)}, u32[]{:S(2)}) collective-permute-start(bf16[1,16,128]{2,1,0:T(8,128)(2,1)} %param.15), channel_id=1, source_target_pairs={{3,0},{0,1},{1,2},{2,3},{7,4},{4,5},{5,6},{6,7},{11,8},{8,9},{9,10... | collective-permute-start | bytes 12296 | tf_op jit(solution)/shard_map/ppermute | solution.py:13
  12.2 24.8 %collective-permute-start = (bf16[1,16]{1,0:T(2,128)(2,1)S(1)}, bf16[1,16]{1,0:T(2,128)(2,1)S(1)}, u32[]{:S(2)}, u32[]{:S(2)}) collective-permute-start(bf16[1,16]{1,0:T(2,128)(2,1)S(1)} %get-tuple-element.33), channel_id=1, source_target_pairs={{3,0},{0,1},{1,2},{2,3},{7,4},{4,5},{5,6},{6,7},{11,8},{8,9},{9,10... | collective-permute-start | bytes 104 | tf_op jit(solution)/shard_map/ppermute | solution.py:13
  13.6 200.5 %all-to-all-start = ((bf16[64,1,16,128]{3,2,1,0:T(8,128)(2,1)}), bf16[64,1,16,128]{3,2,1,0:T(8,128)(2,1)S(1)}, u32[]{:S(2)}, u32[]{:S(2)}) async-start(bf16[64,1,16,128]{3,2,1,0:T(8,128)(2,1)} %stack.8), calls=%async_computation | async-start | bytes 524288 | tf_op jit(solution)/shard_map/all_to_all | solution.py:72
  37.3 3.0 collective-permute-start.2
  40.4 4.5 collective-permute-start.4
  177.5 34.5 %collective-permute-start.3 = (bf16[1,16,128]{2,1,0:T(8,128)(2,1)S(1)}, bf16[1,16,128]{2,1,0:T(8,128)(2,1)S(1)}, u32[]{:S(2)}, u32[]{:S(2)}) collective-permute-start(bf16[1,16,128]{2,1,0:T(8,128)(2,1)S(1)} %collective-permute-done.1), channel_id=1, source_target_pairs={{3,0},{0,1},{1,2},{2,3},{7,4},{4,5},{5,6},{6,7},{11,8},{8,9},{9,10... | collective-permute-start | bytes 12296 | tf_op jit(solution)/shard_map/ppermute | solution.py:13
  212.0 51.0 %collective-permute-start.5 = (bf16[1,16,128]{2,1,0:T(8,128)(2,1)S(1)}, bf16[1,16,128]{2,1,0:T(8,128)(2,1)S(1)}, u32[]{:S(2)}, u32[]{:S(2)}) collective-permute-start(bf16[1,16,128]{2,1,0:T(8,128)(2,1)S(1)} %collective-permute-done.3), channel_id=1, source_target_pairs={{3,0},{0,1},{1,2},{2,3},{7,4},{4,5},{5,6},{6,7},{11,8},{8,9},{9,10... | collective-permute-start | bytes 12296 | tf_op jit(solution)/shard_map/ppermute | solution.py:13
  214.9 17.1 %all-to-all-start.1 = ((bf16[64,1,16,128]{3,2,1,0:T(8,128)(2,1)}), bf16[64,1,16,128]{3,2,1,0:T(8,128)(2,1)S(1)}, u32[]{:S(2)}, u32[]{:S(2)}) async-start(bf16[64,1,16,128]{3,2,1,0:T(8,128)(2,1)} %stack.9), calls=%async_computation.1 | async-start | bytes 524288 | tf_op jit(solution)/shard_map/all_to_all | solution.py:72
  232.8 30.3 %all-to-all-start.2 = ((bf16[64,1,16,128]{3,2,1,0:T(8,128)(2,1)}), bf16[64,1,16,128]{3,2,1,0:T(8,128)(2,1)S(1)}, u32[]{:S(2)}, u32[]{:S(2)}) async-start(bf16[64,1,16,128]{3,2,1,0:T(8,128)(2,1)} %stack.10), calls=%async_computation.2 | async-start | bytes 524288 | tf_op jit(solution)/shard_map/all_to_all | solution.py:72
  254.2 4.4 copy-start.1
  263.8 21.5 %all-to-all-start.3 = ((bf16[64,1,16,128]{3,2,1,0:T(8,128)(2,1)}), bf16[64,1,16,128]{3,2,1,0:T(8,128)(2,1)S(1)}, u32[]{:S(2)}, u32[]{:S(2)}) async-start(bf16[64,1,16,128]{3,2,1,0:T(8,128)(2,1)} %stack.11), calls=%async_computation.3 | async-start | bytes 524288 | tf_op jit(solution)/shard_map/all_to_all | solution.py:72
  274.4 264.5 %all-reduce.7.cloned.1.call-start = ((), (), s32[]{:S(2)}) async-start(), calls=%async_computation.4 | async-start | bytes 131072 | tf_op jit(solution)/shard_map/psum | solution.py:106
Sparse Core Ops, SparseCore 0:
  297.8 241.0 all-reduce.6
